TPU v7x, 32 devices: a whole 2x2x4 slice. The times are simulated.
32 devices in a mesh: src: 2 (over x), tgt: 16 (over z, y, core).
Axes of the slice: x: 2, y: 2, z: 4, core: 2. Of those that a mesh axis runs over, the one named last changes fastest.
Arguments:
- src_emb: bfloat16 [8192, 256], P(('src', 'tgt')), may hold values from -32 to 32
- tgt_emb: bfloat16 [16384, 256], P(('tgt', 'src')), may hold values from -32 to 32
- block_rows: int32 [2, 16, 24], P('src', 'tgt'), may hold values from 0 to 15, as said below
- block_cols: int32 [2, 16, 24], P('src', 'tgt'), may hold values from 0 to 3
- block_counts: int32 [2, 16], P('src', 'tgt'), may hold values from 4 to 24, as said below
Outputs:
- transport: bfloat16 [2, 16, 24, 256, 256], P('src', 'tgt')
- row_potential: float32 [8192], P(('src', 'tgt'))
- col_potential: float32 [16384], P(('tgt', 'src'))
Inputs may be any that keep to these rules, and one draw needn't show every extreme that they name: The 24 slots of one device name distinct blocks (block_rows, block_cols); its first 4 slots name every local block column once; every local block row of a src index is named by a live slot of some device of that index. `block_counts`: exactly 24 on some device.
All inputs are finite; a program needn't handle non-finite values.
Results may differ from a plain program's by a relative error of at most 0.0019.
The roundings to bfloat16 on the way count: a program that leaves them out, or rounds other values in their place, can miss the bound.
Values may be sent and summed in bfloat16 or wider, within the bound.
No kernel may reach another device: no remote copies, remote signals or barrier semaphores. Data moves between devices by JAX's collectives and lax.ppermute only.
A program may use at most 64 MiB of HBM per device.

v0:
```python
import math
import jax
import jax.numpy as jnp
from jax import lax
from jax.sharding import PartitionSpec as P

DIM = 256
BLOCK = 256
ROW_BLOCKS = 16
COL_BLOCKS = 4
SLOTS = 24
ITERS = 3
inv_temp = 250.0
sentinel = -1e30
highest = lax.Precision.HIGHEST


def unit_rows(embedding):
    values = embedding.astype(jnp.float32)
    inverse_norm = lax.rsqrt(jnp.sum(values * values, axis=1, keepdims=True) + 1e-06)
    return (values * inverse_norm).astype(jnp.bfloat16)


def spread_top(slot_top, slot_hot):
    return jnp.max(jnp.where(slot_hot[:, :, None] > 0, slot_top[:, None, :], sentinel), axis=0)


def spread_sum(slot_sums, slot_hot):
    return jnp.einsum("cn,cb->nb", slot_hot, slot_sums, precision=highest)


def row_potential(scores, col_slots, rows_idx, row_hot):
    shifted = scores + col_slots[:, None, :]
    top_local = spread_top(jnp.max(shifted, axis=2), row_hot)
    top_value = lax.pmax(top_local, "tgt")
    slot_sums = jnp.sum(jnp.exp(shifted - top_value[rows_idx][:, :, None]), axis=2)
    sum_total = lax.psum(spread_sum(slot_sums, row_hot), "tgt")
    row_dual = -(top_value + jnp.log(sum_total))
    share_width = row_dual.size // lax.axis_size("tgt")
    own_rows = lax.dynamic_slice_in_dim(
        row_dual.reshape(-1), lax.axis_index("tgt") * share_width, share_width
    )
    return (row_dual, own_rows)


def col_potential(scores, row_slots, cols_idx, col_hot, log_ratio):
    shifted = scores + row_slots[:, :, None]
    top_local = spread_top(jnp.max(shifted, axis=1), col_hot)
    top_value = lax.pmax(top_local, "src")
    slot_sums = jnp.sum(jnp.exp(shifted - top_value[cols_idx][:, None, :]), axis=1)
    sum_total = lax.psum(spread_sum(slot_sums, col_hot), "src")
    return log_ratio - (top_value + jnp.log(sum_total))


def shards(src_emb, tgt_emb, block_rows, block_cols, block_counts):
    src_rows = lax.all_gather(unit_rows(src_emb), "tgt", axis=0, tiled=True)
    tgt_rows = lax.all_gather(unit_rows(tgt_emb), "src", axis=0, tiled=True)
    rows_idx = block_rows[0, 0]
    cols_idx = block_cols[0, 0]
    live_slot = jnp.arange(SLOTS, dtype=jnp.int32) < block_counts[0, 0]
    row_hot = (
        (rows_idx[:, None] == jnp.arange(ROW_BLOCKS, dtype=jnp.int32)[None, :]) & live_slot[:, None]
    ).astype(jnp.float32)
    col_hot = (
        (cols_idx[:, None] == jnp.arange(COL_BLOCKS, dtype=jnp.int32)[None, :]) & live_slot[:, None]
    ).astype(jnp.float32)
    src_blocks = src_rows.reshape(ROW_BLOCKS, BLOCK, DIM)[rows_idx]
    tgt_blocks = tgt_rows.reshape(COL_BLOCKS, BLOCK, DIM)[cols_idx]
    products = jnp.einsum(
        "cbe,cde->cbd", src_blocks, tgt_blocks, preferred_element_type=jnp.float32
    )
    scores = jnp.where(live_slot[:, None, None], products * inv_temp, sentinel)
    log_ratio = math.log(ROW_BLOCKS * lax.axis_size("src") / (COL_BLOCKS * lax.axis_size("tgt")))
    col_dual = jnp.zeros((COL_BLOCKS, BLOCK), jnp.float32)
    row_dual = jnp.zeros((ROW_BLOCKS, BLOCK), jnp.float32)
    own_rows = jnp.zeros((ROW_BLOCKS * BLOCK // lax.axis_size("tgt"),), jnp.float32)
    for sweep in range(ITERS):
        row_dual, own_rows = row_potential(scores, col_dual[cols_idx], rows_idx, row_hot)
        col_dual = col_potential(scores, row_dual[rows_idx], cols_idx, col_hot, log_ratio)
    transport = jnp.exp(
        scores + row_dual[rows_idx][:, :, None] + col_dual[cols_idx][:, None, :]
    ).astype(jnp.bfloat16)
    share_width = col_dual.size // lax.axis_size("src")
    own_cols = lax.dynamic_slice_in_dim(
        col_dual.reshape(-1), lax.axis_index("src") * share_width, share_width
    )
    return (transport[None, None], own_rows / inv_temp, own_cols / inv_temp)


def solution(mesh):
    return jax.shard_map(
        shards,
        mesh=mesh,
        in_specs=(
            P(("src", "tgt"), None),
            P(("tgt", "src"), None),
            P("src", "tgt", None),
            P("src", "tgt", None),
            P("src", "tgt"),
        ),
        out_specs=(P("src", "tgt", None, None, None), P(("src", "tgt")), P(("tgt", "src"))),
        check_vma=False,
    )
```

profile of v0, /device:TPU:0, one launch (start us, length us, event | category | flops | bytes accessed | tf_op | source)
XLA Modules:
  0.0 503.7 jit_solution(15820733972963911582)
XLA Ops:
  7.2 1.0 fusion.3
  8.3 1.7 fusion.4
  10.0 0.7 fusion.20
  10.6 0.6 gather_fusion.2
  11.2 1.1 fusion.1
  12.3 1.1 fusion.2
  13.4 9.9 %all_gather.7 = bf16[1024,256]{1,0:T(8,128)(2,1)S(1)} all-gather(bf16[512,256]{1,0:T(8,128)(2,1)S(1)} %fusion.2), channel_id=1, replica_groups=mesh['src'=2,'tgt'=16] {'src'}, dimensions={0}, use_global_device_ids=true | all-gather | bytes 786432 | tf_op jit(solution)/shard_map/all_gather | solution.py:57
  23.4 2.5 gather_fusion.1
  26.8 28.1 %all-gather.2.cloned.1.call-done = bf16[4096,256]{1,0:T(8,128)(2,1)} async-done(((bf16[256,256]{1,0:T(8,128)(2,1)}), bf16[4096,256]{1,0:T(8,128)(2,1)}) %all-gather.2.cloned.1.call-update) | async-done | bytes 2097168 | tf_op jit(solution)/shard_map/all_gather | solution.py:56
  54.9 4.1 gather_fusion
  59.0 5.9 %add_reduce_fusion.4 = (f32[24,256]{1,0:T(8,128)S(1)}, f32[24,256,256]{2,1,0:T(8,128)}) fusion(f32[24,256]{1,0:T(8,128)S(1)} %gather_fusion.2, bf16[24,256,256]{2,1,0:T(8,128)(2,1)} %gather_fusion, bf16[24,256,256]{2,1,0:T(8,128)(2,1)S(1)} %copy-done, pred[24]{0:T(512)(128)(4,1)S(1)} %iota_compare_fusion.2), kind=kOutput, calls=%fused_computation.27 | convolution fusion | flops 811591680 | bytes 12632088 | tf_op jit(solution)/shard_map/cbe,cde->cbd/dot_general | solution.py:69
  65.0 59.4 %pmax.42 = f32[16,256]{1,0:T(8,128)S(1)} all-reduce(f32[16,256]{1,0:T(8,128)S(1)} %select_reduce_fusion.2), channel_id=1, replica_groups=mesh['src'=2,'tgt'=16] {'tgt'}, use_global_device_ids=true, to_apply=%region_4.5 | all-reduce | flops 4096 | bytes 32768 | tf_op jit(solution)/shard_map/pmax | solution.py:35
  124.4 0.6 gather_fusion.3
  125.0 3.9 exponential_reduce_fusion.5
  129.2 57.6 %psum.42 = f32[16,256]{1,0:T(8,128)S(1)} all-reduce(f32[16,256]{1,0:T(8,128)S(1)} %fusion.10), channel_id=1, replica_groups=mesh['src'=2,'tgt'=16] {'tgt'}, use_global_device_ids=true, to_apply=%region_6.7 | all-reduce | flops 4096 | bytes 32768 | tf_op jit(solution)/shard_map/psum | solution.py:37
  186.8 0.6 gather_fusion.4
  187.4 3.4 add_reduce_fusion.3
  190.9 4.9 pmax.43
  195.8 0.6 gather_fusion.5
  196.4 3.6 exponential_reduce_fusion.4
  200.1 4.9 psum.43
  205.0 0.6 gather_fusion.6
  205.6 3.7 add_reduce_fusion.2
  209.4 57.6 %pmax.44 = f32[16,256]{1,0:T(8,128)S(1)} all-reduce(f32[16,256]{1,0:T(8,128)S(1)} %select_reduce_fusion.1), channel_id=1, replica_groups=mesh['src'=2,'tgt'=16] {'tgt'}, use_global_device_ids=true, to_apply=%region_14.15 | all-reduce | flops 4096 | bytes 32768 | tf_op jit(solution)/shard_map/pmax | solution.py:35
  267.0 0.6 gather_fusion.7
  267.6 3.9 exponential_reduce_fusion.3
  271.7 57.6 %psum.44 = f32[16,256]{1,0:T(8,128)S(1)} all-reduce(f32[16,256]{1,0:T(8,128)S(1)} %fusion.8), channel_id=1, replica_groups=mesh['src'=2,'tgt'=16] {'tgt'}, use_global_device_ids=true, to_apply=%region_16.17 | all-reduce | flops 4096 | bytes 32768 | tf_op jit(solution)/shard_map/psum | solution.py:37
  329.4 0.6 gather_fusion.8
  330.0 3.4 add_reduce_fusion.1
  333.4 4.9 pmax.45
  338.4 0.6 gather_fusion.9
  339.0 3.6 exponential_reduce_fusion.2
  342.6 4.9 psum.45
  347.6 0.6 gather_fusion.10
  348.2 3.7 add_reduce_fusion
  352.0 57.8 %pmax.46 = f32[16,256]{1,0:T(8,128)S(1)} all-reduce(f32[16,256]{1,0:T(8,128)S(1)} %select_reduce_fusion), channel_id=1, replica_groups=mesh['src'=2,'tgt'=16] {'tgt'}, use_global_device_ids=true, to_apply=%region_24.25 | all-reduce | flops 4096 | bytes 32768 | tf_op jit(solution)/shard_map/pmax | solution.py:35
  410.4 3.9 exponential_reduce_fusion.1
  414.5 57.6 %psum.46 = f32[16,256]{1,0:T(8,128)S(1)} all-reduce(f32[16,256]{1,0:T(8,128)S(1)} %fusion.6), channel_id=1, replica_groups=mesh['src'=2,'tgt'=16] {'tgt'}, use_global_device_ids=true, to_apply=%region_26.27 | all-reduce | flops 4096 | bytes 32768 | tf_op jit(solution)/shard_map/psum | solution.py:37
  472.1 0.6 gather_fusion.12
  472.7 3.4 add_reduce_fusion.5
  476.2 4.9 pmax.47
  481.1 0.6 gather_fusion.13
  481.7 3.6 exponential_reduce_fusion
  485.4 4.9 psum.47
  490.3 0.6 gather_fusion.14
  490.9 4.6 fusion
  495.5 0.7 dynamic-slice_multiply_fusion
  496.2 0.6 dynamic-slice_multiply_fusion.1
  (38 shorter events, 2.6 us)
Async XLA Ops:
  7.2 19.6 %copy-start.1 = (s32[1,1,24]{2,1,0:T(1,128)S(1)}, s32[1,1,24]{2,1,0:T(1,128)}, u32[]{:S(2)}) copy-start(s32[1,1,24]{2,1,0:T(1,128)} %param.8) | copy-start | bytes 292
  7.2 19.5 %copy-start.2 = (s32[1,1,24]{2,1,0:T(1,128)S(1)}, s32[1,1,24]{2,1,0:T(1,128)}, u32[]{:S(2)}) copy-start(s32[1,1,24]{2,1,0:T(1,128)} %param.7) | copy-start | bytes 292
  7.2 47.8 %all-gather.2.cloned.1.call-start = ((), (), s32[]{:S(2)}) async-start(), calls=%async_computation | async-start | bytes 2228224 | tf_op jit(solution)/shard_map/all_gather | solution.py:56
  25.9 33.2 %copy-start = (bf16[24,256,256]{2,1,0:T(8,128)(2,1)S(1)}, bf16[24,256,256]{2,1,0:T(8,128)(2,1)}, u32[]{:S(2)}) copy-start(bf16[24,256,256]{2,1,0:T(8,128)(2,1)} %gather_fusion.1) | copy-start | bytes 9437188
Sparse Core Ops, SparseCore 0:
  10.7 44.1 all-gather.1
where the time goes:
time: 504 us
  blocking collectives  387 us (77%)
  other arithmetic  51.9 us (10%)
  waiting for transfers between devices  28.1 us (6%)
  between operations  15.1 us (3%)
  local copies, waits for them, and re-layouts  14.3 us (3%)
  matrix products  7.02 us (1%)
    pmax x3, blocking collectives, row_potential(): top_value = lax.pmax(top_local, 'tgt')  175 us
    psum x3, blocking collectives, row_potential(): sum_total = lax.psum(spread_sum(slot_sums, row_hot), 'tgt')  173 us
    all_gather x1, waiting for transfers between devices, shards(): src_rows = lax.all_gather(unit_rows(src_emb), 'tgt', axis=0, tiled=True)  28.1 us
    pmax x3, blocking collectives, col_potential(): top_value = lax.pmax(top_local, 'src')  14.8 us
    psum x3, blocking collectives, col_potential(): sum_total = lax.psum(spread_sum(slot_sums, col_hot), 'src')  14.8 us
    reduce_sum x3, other arithmetic, row_potential(): jnp.sum(jnp.exp(shifted - top_value[rows_idx][:, :, None]), axis=2)  11.6 us
    reduce_sum x3, other arithmetic, col_potential(): jnp.sum(jnp.exp(shifted - top_value[cols_idx][:, None, :]), axis=1)  10.7 us
    reduce_max x3, other arithmetic, col_potential(): top_local = spread_top(jnp.max(shifted, axis=1), col_hot)  10.1 us
  transfers between devices with their start and end apart: 1, of which 1 were waited for; matrix products, arithmetic and copies ran while one was open for 1% of the time, Pallas kernels for 0%

commit v1 on v0

--- a/solution.py
+++ b/solution.py
@@ -34,7 +34,11 @@
     top_local = spread_top(jnp.max(shifted, axis=2), row_hot)
     top_value = lax.pmax(top_local, "tgt")
     slot_sums = jnp.sum(jnp.exp(shifted - top_value[rows_idx][:, :, None]), axis=2)
-    sum_total = lax.psum(spread_sum(slot_sums, row_hot), "tgt")
+
+    def prepare_packet_on(a0, which_axis):
+        return lax.all_gather(a0, which_axis).sum(axis=0)
+
+    sum_total = prepare_packet_on(spread_sum(slot_sums, row_hot), "tgt")
     row_dual = -(top_value + jnp.log(sum_total))
     share_width = row_dual.size // lax.axis_size("tgt")
     own_rows = lax.dynamic_slice_in_dim(

time: 504 us -> 385 us (0.76)
  blocking collectives: 387 us -> 268 us
    psum x3 -> x0, blocking collectives: 173 us -> none  [row_potential(): sum_total = lax.psum(spread_sum(slot_sums, row_hot), 'tgt')]
    all_gather x0 -> x3, blocking collectives: none -> 53.5 us  [prepare_packet_on(): return lax.all_gather(a0, which_axis).sum(axis=0)]
  transfers between devices with their start and end apart: 1 -> 1, of which waited for: 1 -> 1; matrix products, arithmetic and copies ran while one was open for 1% -> 2% of each run, Pallas kernels for 0% -> 0%
where the time goes in v1:
time: 385 us; the launch traced here: 384 us
  blocking collectives  268 us (70%)
  other arithmetic  52 us (14%)
  waiting for transfers between devices  28.1 us (7%)
  between operations  15.1 us (4%)
  local copies, waits for them, and re-layouts  14.3 us (4%)
  matrix products  7.02 us (2%)
    pmax x3, blocking collectives, row_potential(): top_value = lax.pmax(top_local, 'tgt')  175 us
    all_gather x3, blocking collectives, prepare_packet_on(): return lax.all_gather(a0, which_axis).sum(axis=0)  53.5 us
    all_gather x1, waiting for transfers between devices, shards(): src_rows = lax.all_gather(unit_rows(src_emb), 'tgt', axis=0, tiled=True)  28.1 us
    pmax x3, blocking collectives, col_potential(): top_value = lax.pmax(top_local, 'src')  14.8 us
    psum x3, blocking collectives, col_potential(): sum_total = lax.psum(spread_sum(slot_sums, col_hot), 'src')  14.8 us
    reduce_sum x3, other arithmetic, row_potential(): jnp.sum(jnp.exp(shifted - top_value[rows_idx][:, :, None]), axis=2)  11.6 us
    reduce_sum x3, other arithmetic, col_potential(): jnp.sum(jnp.exp(shifted - top_value[cols_idx][:, None, :]), axis=1)  10.7 us
    reduce_max x3, other arithmetic, col_potential(): top_local = spread_top(jnp.max(shifted, axis=1), col_hot)  10.1 us
  transfers between devices with their start and end apart: 1, of which 1 were waited for; matrix products, arithmetic and copies ran while one was open for 2% of the time, Pallas kernels for 0%

profile of v1, /device:TPU:0, one launch (start us, length us, event | category | flops | bytes accessed | tf_op | source)
XLA Modules:
  0.0 384.4 jit_solution(148279379508810752)
XLA Ops:
  7.2 1.0 fusion.3
  8.3 1.7 fusion.4
  10.0 0.7 fusion.20
  10.6 0.6 gather_fusion.2
  11.2 1.1 fusion.1
  12.3 1.1 fusion.2
  13.4 9.9 %all_gather.25 = bf16[1024,256]{1,0:T(8,128)(2,1)S(1)} all-gather(bf16[512,256]{1,0:T(8,128)(2,1)S(1)} %fusion.2), channel_id=1, replica_groups=mesh['src'=2,'tgt'=16] {'src'}, dimensions={0}, use_global_device_ids=true | all-gather | bytes 786432 | tf_op jit(solution)/shard_map/all_gather | solution.py:61
  23.4 2.5 gather_fusion.1
  26.8 28.1 %all-gather.5.cloned.1.call-done = bf16[4096,256]{1,0:T(8,128)(2,1)} async-done(((bf16[256,256]{1,0:T(8,128)(2,1)}), bf16[4096,256]{1,0:T(8,128)(2,1)}) %all-gather.5.cloned.1.call-update) | async-done | bytes 2097168 | tf_op jit(solution)/shard_map/all_gather | solution.py:60
  54.9 4.1 %gather_fusion = bf16[24,256,256]{2,1,0:T(8,128)(2,1)} fusion(bf16[16,256,256]{2,1,0:T(8,128)(2,1)} %bitcast.36, s32[1024]{0:T(1024)S(1)} %pad_clamp_fusion.1), kind=kCustom, calls=%fused_computation | custom fusion | bytes 6291552 | tf_op jit(solution)/shard_map/gather | solution.py:71
  59.0 5.9 %add_reduce_fusion.4 = (f32[24,256]{1,0:T(8,128)S(1)}, f32[24,256,256]{2,1,0:T(8,128)}) fusion(f32[24,256]{1,0:T(8,128)S(1)} %gather_fusion.2, bf16[24,256,256]{2,1,0:T(8,128)(2,1)} %gather_fusion, bf16[24,256,256]{2,1,0:T(8,128)(2,1)S(1)} %copy-done, pred[24]{0:T(512)(128)(4,1)S(1)} %iota_compare_fusion.2), kind=kOutput, calls=%fused_computation.27 | convolution fusion | flops 811591680 | bytes 12632088 | tf_op jit(solution)/shard_map/cbe,cde->cbd/dot_general | solution.py:73
  65.0 59.4 %pmax.42 = f32[16,256]{1,0:T(8,128)S(1)} all-reduce(f32[16,256]{1,0:T(8,128)S(1)} %select_reduce_fusion.2), channel_id=1, replica_groups=mesh['src'=2,'tgt'=16] {'tgt'}, use_global_device_ids=true, to_apply=%region_4.5 | all-reduce | flops 4096 | bytes 32768 | tf_op jit(solution)/shard_map/pmax | solution.py:35
  124.4 0.6 gather_fusion.3
  125.0 3.9 %exponential_reduce_fusion.5 = f32[24,256]{1,0:T(8,128)S(1)} fusion(f32[24,256,256]{2,1,0:T(8,128)} %get-tuple-element.6, f32[24,256]{1,0:T(8,128)S(1)} %gather_fusion.3, f32[24,256]{1,0:T(8,128)S(1)} %gather_fusion.2), kind=kLoop, calls=%fused_computation.21 | loop fusion | flops 4712448 | bytes 6365184 | tf_op jit(solution)/shard_map/reduce_sum | solution.py:36
  129.2 17.8 %all-gather = f32[256,256]{1,0:T(8,128)S(1)} all-gather(f32[16,256]{1,0:T(8,128)S(1)} %fusion.10), channel_id=2, replica_groups=mesh['src'=2,'tgt'=16] {'tgt'}, dimensions={0}, use_global_device_ids=true | all-gather | bytes 278528 | tf_op jit(solution)/shard_map/all_gather | solution.py:39
  147.0 0.6 gather_fusion.4
  147.6 3.4 add_reduce_fusion.3
  151.1 4.9 %pmax.43 = f32[4,256]{1,0:T(4,128)S(1)} all-reduce(f32[4,256]{1,0:T(4,128)S(1)} %select_reduce_fusion.5), channel_id=1, replica_groups=mesh['src'=2,'tgt'=16] {'src'}, use_global_device_ids=true, to_apply=%region_9.10 | all-reduce | flops 1024 | bytes 8192 | tf_op jit(solution)/shard_map/pmax | solution.py:53
  156.0 0.6 gather_fusion.5
  156.6 3.6 exponential_reduce_fusion.4
  160.3 4.9 %psum.21 = f32[4,256]{1,0:T(4,128)S(1)} all-reduce(f32[4,256]{1,0:T(4,128)S(1)} %fusion.22), channel_id=1, replica_groups=mesh['src'=2,'tgt'=16] {'src'}, use_global_device_ids=true, to_apply=%region_11.12 | all-reduce | flops 1024 | bytes 8192 | tf_op jit(solution)/shard_map/psum | solution.py:55
  165.3 0.6 gather_fusion.6
  165.8 3.7 add_reduce_fusion.2
  169.7 57.6 %pmax.44 = f32[16,256]{1,0:T(8,128)S(1)} all-reduce(f32[16,256]{1,0:T(8,128)S(1)} %select_reduce_fusion.1), channel_id=1, replica_groups=mesh['src'=2,'tgt'=16] {'tgt'}, use_global_device_ids=true, to_apply=%region_14.15 | all-reduce | flops 4096 | bytes 32768 | tf_op jit(solution)/shard_map/pmax | solution.py:35
  227.3 0.6 gather_fusion.7
  227.9 3.9 %exponential_reduce_fusion.3 = f32[24,256]{1,0:T(8,128)S(1)} fusion(f32[24,256,256]{2,1,0:T(8,128)} %get-tuple-element.6, f32[24,256]{1,0:T(8,128)S(1)} %gather_fusion.7, f32[24,256]{1,0:T(8,128)S(1)} %gather_fusion.6), kind=kLoop, calls=%fused_computation.19 | loop fusion | flops 4712448 | bytes 6365184 | tf_op jit(solution)/shard_map/reduce_sum | solution.py:36
  232.0 17.8 %all-gather.1 = f32[256,256]{1,0:T(8,128)S(1)} all-gather(f32[16,256]{1,0:T(8,128)S(1)} %fusion.8), channel_id=3, replica_groups=mesh['src'=2,'tgt'=16] {'tgt'}, dimensions={0}, use_global_device_ids=true | all-gather | bytes 278528 | tf_op jit(solution)/shard_map/all_gather | solution.py:39
  249.9 0.6 gather_fusion.8
  250.5 3.4 add_reduce_fusion.1
  253.9 4.9 %pmax.45 = f32[4,256]{1,0:T(4,128)S(1)} all-reduce(f32[4,256]{1,0:T(4,128)S(1)} %select_reduce_fusion.4), channel_id=1, replica_groups=mesh['src'=2,'tgt'=16] {'src'}, use_global_device_ids=true, to_apply=%region_19.20 | all-reduce | flops 1024 | bytes 8192 | tf_op jit(solution)/shard_map/pmax | solution.py:53
  258.9 0.6 gather_fusion.9
  259.5 3.6 exponential_reduce_fusion.2
  263.1 4.9 %psum.22 = f32[4,256]{1,0:T(4,128)S(1)} all-reduce(f32[4,256]{1,0:T(4,128)S(1)} %fusion.23), channel_id=1, replica_groups=mesh['src'=2,'tgt'=16] {'src'}, use_global_device_ids=true, to_apply=%region_21.22 | all-reduce | flops 1024 | bytes 8192 | tf_op jit(solution)/shard_map/psum | solution.py:55
  268.1 0.6 gather_fusion.10
  268.7 3.7 add_reduce_fusion
  272.5 57.8 %pmax.46 = f32[16,256]{1,0:T(8,128)S(1)} all-reduce(f32[16,256]{1,0:T(8,128)S(1)} %select_reduce_fusion), channel_id=1, replica_groups=mesh['src'=2,'tgt'=16] {'tgt'}, use_global_device_ids=true, to_apply=%region_24.25 | all-reduce | flops 4096 | bytes 32768 | tf_op jit(solution)/shard_map/pmax | solution.py:35
  330.9 3.9 %exponential_reduce_fusion.1 = f32[24,256]{1,0:T(8,128)S(1)} fusion(f32[24,256,256]{2,1,0:T(8,128)} %get-tuple-element.6, f32[24,256]{1,0:T(8,128)S(1)} %gather_fusion.11, f32[24,256]{1,0:T(8,128)S(1)} %gather_fusion.10), kind=kLoop, calls=%fused_computation.17 | loop fusion | flops 4712448 | bytes 6365184 | tf_op jit(solution)/shard_map/reduce_sum | solution.py:36
  335.0 17.8 %all-gather.2 = f32[256,256]{1,0:T(8,128)S(1)} all-gather(f32[16,256]{1,0:T(8,128)S(1)} %fusion.6), channel_id=4, replica_groups=mesh['src'=2,'tgt'=16] {'tgt'}, dimensions={0}, use_global_device_ids=true | all-gather | bytes 278528 | tf_op jit(solution)/shard_map/all_gather | solution.py:39
  352.9 0.6 gather_fusion.12
  353.5 3.4 add_reduce_fusion.5
  356.9 4.9 %pmax.47 = f32[4,256]{1,0:T(4,128)S(1)} all-reduce(f32[4,256]{1,0:T(4,128)S(1)} %select_reduce_fusion.3), channel_id=1, replica_groups=mesh['src'=2,'tgt'=16] {'src'}, use_global_device_ids=true, to_apply=%region_29.30 | all-reduce | flops 1024 | bytes 8192 | tf_op jit(solution)/shard_map/pmax | solution.py:53
  361.9 0.6 gather_fusion.13
  362.5 3.6 exponential_reduce_fusion
  366.2 4.9 %psum.23 = f32[4,256]{1,0:T(4,128)S(1)} all-reduce(f32[4,256]{1,0:T(4,128)S(1)} %fusion.24), channel_id=1, replica_groups=mesh['src'=2,'tgt'=16] {'src'}, use_global_device_ids=true, to_apply=%region_31.32 | all-reduce | flops 1024 | bytes 8192 | tf_op jit(solution)/shard_map/psum | solution.py:55
  371.1 0.6 gather_fusion.14
  371.7 4.6 %fusion = bf16[1,1,24,256,256]{4,3,2,1,0:T(8,128)(2,1)} fusion(f32[24,256,256]{2,1,0:T(8,128)} %get-tuple-element.6, f32[24,256]{1,0:T(8,128)S(1)} %gather_fusion.14, f32[24,256]{1,0:T(8,128)S(1)} %gather_fusion.12), kind=kLoop, calls=%fused_computation.29 | loop fusion | flops 4718592 | bytes 9486336 | tf_op jit(solution)/shard_map/broadcast_in_dim | solution.py:91
  376.3 0.7 dynamic-slice_multiply_fusion
  376.9 0.6 dynamic-slice_multiply_fusion.1
  (41 shorter events, 2.7 us)
Async XLA Ops:
  7.2 19.6 %copy-start.1 = (s32[1,1,24]{2,1,0:T(1,128)S(1)}, s32[1,1,24]{2,1,0:T(1,128)}, u32[]{:S(2)}) copy-start(s32[1,1,24]{2,1,0:T(1,128)} %param.8) | copy-start | bytes 292
  7.2 19.5 %copy-start.2 = (s32[1,1,24]{2,1,0:T(1,128)S(1)}, s32[1,1,24]{2,1,0:T(1,128)}, u32[]{:S(2)}) copy-start(s32[1,1,24]{2,1,0:T(1,128)} %param.7) | copy-start | bytes 292
  7.2 47.8 %all-gather.5.cloned.1.call-start = ((), (), s32[]{:S(2)}) async-start(), calls=%async_computation | async-start | bytes 2228224 | tf_op jit(solution)/shard_map/all_gather | solution.py:60
  25.9 33.2 %copy-start = (bf16[24,256,256]{2,1,0:T(8,128)(2,1)S(1)}, bf16[24,256,256]{2,1,0:T(8,128)(2,1)}, u32[]{:S(2)}) copy-start(bf16[24,256,256]{2,1,0:T(8,128)(2,1)} %gather_fusion.1) | copy-start | bytes 9437188
Sparse Core Ops, SparseCore 0:
  10.7 44.1 all-gather.4
